TPU v7x, 32 devices: a whole 2x2x4 slice. The times are simulated.
32 devices in a mesh: tm: 8 (over z, y), slab: 4 (over x, core).
Axes of the slice: x: 2, y: 2, z: 4, core: 2. Of those that a mesh axis runs over, the one named last changes fastest.
Arguments:
- features: bfloat16 [8, 6144, 256], P('tm', 'slab'), may hold values from -6 to 6
- ref_lists: int32 [8, 4, 16], P('tm'), may hold values from 0 to 11
- tile_rows: int32 [8, 128], P('tm', 'slab'), may hold values from 0 to 11
- tile_sources: int32 [8, 128], P('tm', 'slab'), may hold values from 0 to 15
- tile_counts: int32 [8, 4], P('tm', 'slab'), may hold values from 9 to 32
- tile_values: bfloat16 [8, 128, 128, 128], P('tm', 'slab'), may hold values from -0.3125 to 0.3125
- w_input: bfloat16 [2, 256, 1024], replicated, may hold values from -0.375 to 0.375
- w_hidden: bfloat16 [2, 256, 1024], replicated, may hold values from -0.375 to 0.375
- bias: float32 [2, 1024], replicated, may hold values from -4 to 4
Outputs:
- hidden_out: bfloat16 [8, 6144, 256], P('tm', 'slab')
Inputs may be any that keep to these rules, and one draw needn't show every extreme that they name: `ref_lists`: row tile indices within a slab. `tile_counts`: slots at or after the count are ignored.
All inputs are finite; a program needn't handle non-finite values.
Results may differ from a plain program's by a relative error of at most 0.0055.
Values may be sent and summed in bfloat16 or wider, within the bound.
No kernel may reach another device: no remote copies, remote signals or barrier semaphores. Data moves between devices by JAX's collectives and lax.ppermute only.
A program may use at most 64 MiB of HBM per device.

v0:
```python
import jax
import jax.numpy as jnp
from jax import lax
from jax.sharding import PartitionSpec as P


def lstm_run(inputs, weight_in, weight_rec, gate_bias):
    steps_count, vertex_count, feature_width = inputs.shape
    projected = jnp.dot(
        inputs.reshape(-1, feature_width), weight_in, preferred_element_type=jnp.float32
    )
    projected = projected.reshape(steps_count, vertex_count, -1) + gate_bias
    unit_count = weight_rec.shape[0]

    def advance(state, gate_input):
        hidden, memory = state
        gate_sum = gate_input + jnp.dot(hidden, weight_rec, preferred_element_type=jnp.float32)
        in_gate, forget, candidate, out_gate = jnp.split(gate_sum, 4, axis=-1)
        memory = jax.nn.sigmoid(forget) * memory + jax.nn.sigmoid(in_gate) * jnp.tanh(candidate)
        hidden = (jax.nn.sigmoid(out_gate) * jnp.tanh(memory)).astype(jnp.bfloat16)
        return ((hidden, memory), hidden)

    start_state = (
        jnp.zeros((vertex_count, unit_count), jnp.bfloat16),
        jnp.zeros((vertex_count, unit_count), jnp.float32),
    )
    final_state, outputs = lax.scan(advance, start_state, projected, unroll=4)
    return outputs


def local(
    features, ref_lists, tile_rows, tile_sources, tile_counts, tile_values, w_input, w_hidden, bias
):
    current = features[0]
    row_count, feature_width = current.shape
    tile_size = tile_values.shape[2]
    slot_count = tile_values.shape[1]
    row_tiles = row_count // tile_size
    slab_count = lax.axis_size("slab")
    group_count = lax.axis_size("tm")
    slab_index = lax.axis_index("slab")
    ref_table = ref_lists[0]
    list_length = ref_table.shape[1] // slab_count
    weight_tiles = tile_values[0]
    sources = tile_sources[0]
    live = jnp.arange(slot_count, dtype=jnp.int32) < tile_counts[0, 0]
    one_hot = (tile_rows[0][None, :] == jnp.arange(row_tiles, dtype=jnp.int32)[:, None]) & live[
        None, :
    ]
    one_hot = one_hot.astype(jnp.float32)
    for layer_index in range(w_input.shape[0]):
        wanted = lax.dynamic_slice_in_dim(ref_table, slab_index * list_length, list_length, 1)
        own_tiles = current.reshape(row_tiles, tile_size, -1)
        outgoing = jnp.take(own_tiles, wanted.reshape(-1), axis=0).reshape(
            slab_count, list_length, tile_size, -1
        )
        arrived = lax.all_to_all(outgoing, "slab", split_axis=0, concat_axis=0, tiled=True)
        arrived = arrived.reshape(slab_count * list_length, tile_size, -1)
        picked = jnp.take(arrived, sources, axis=0)
        products = jnp.einsum(
            "kij,kjf->kif", weight_tiles, picked, preferred_element_type=jnp.float32
        )
        mixed = jnp.einsum("rk,kif->rif", one_hot, products).astype(jnp.bfloat16)
        grouped = mixed.reshape(group_count, row_count // group_count, -1)

        def recur(vertex_part, layer_index=layer_index):
            states = lstm_run(
                vertex_part, w_input[layer_index], w_hidden[layer_index], bias[layer_index]
            )
            return lax.all_to_all(states, "tm", split_axis=0, concat_axis=0, tiled=True)

        current = recur(
            lax.all_to_all(grouped, "tm", split_axis=0, concat_axis=0, tiled=True)
        ).reshape(row_count, -1)
    return current[None]


def solution(mesh):
    in_specs = (
        P("tm", "slab", None),
        P("tm", None, None),
        P("tm", "slab"),
        P("tm", "slab"),
        P("tm", "slab"),
        P("tm", "slab", None, None),
        P(),
        P(),
        P(),
    )
    out_specs = P("tm", "slab", None)
    return jax.shard_map(local, mesh=mesh, in_specs=in_specs, out_specs=out_specs, check_vma=False)
```

profile of v0, /device:TPU:0, one launch (start us, length us, event | category | flops | bytes accessed | tf_op | source)
XLA Modules:
  0.0 204.1 jit_solution(12420185842484775039)
XLA Ops:
  0.0 0.8 constant_dynamic-slice_fusion
  1.0 1.7 gather_fusion
  2.7 1.1 broadcast_select_fusion
  3.9 4.2 %all-to-all-start = ((bf16[4,4,128,256]{3,2,1,0:T(8,128)(2,1)}), bf16[4,4,128,256]{3,2,1,0:T(8,128)(2,1)S(1)}, u32[]{:S(2)}, u32[]{:S(2)}) async-start(bf16[4,4,128,256]{3,2,1,0:T(8,128)(2,1)} %bitcast.194), calls=%async_computation | async-start | bytes 2097152 | tf_op jit(solution)/shard_map/all_to_all | solution.py:57
  8.8 13.7 %all-to-all-done = bf16[4,4,128,256]{3,2,1,0:T(8,128)(2,1)S(1)} async-done(((bf16[4,4,128,256]{3,2,1,0:T(8,128)(2,1)}), bf16[4,4,128,256]{3,2,1,0:T(8,128)(2,1)S(1)}, u32[]{:S(2)}, u32[]{:S(2)}) %all-to-all-start) | async-done | bytes 1048608 | tf_op jit(solution)/shard_map/all_to_all | solution.py:57
  22.5 2.0 gather_fusion.1
  24.5 3.8 %fusion.128 = bf16[32,256,128]{2,1,0:T(8,128)(2,1)} fusion(bf16[32,128,256]{2,1,0:T(8,128)(2,1)} %gather_fusion.1, pred[32]{0:T(512)(128)(4,1)S(1)} %compare_and_fusion, bf16[1,32,128,128]{3,2,1,0:T(8,128)(2,1)S(1)} %copy-done), kind=kOutput, calls=%fused_computation.184 | convolution fusion | flops 269484032 | bytes 5242912 | tf_op jit(solution)/shard_map/kij,kjf->kif/dot_general | solution.py:60
  28.3 4.6 %copy.12 = bf16[32,256,128]{1,0,2:T(8,128)(2,1)} copy(bf16[32,256,128]{2,1,0:T(8,128)(2,1)} %fusion.128) | data formatting | bytes 4194304 | tf_op jit(solution)/shard_map/kij,kjf->kif/dot_general | solution.py:60
  32.9 2.0 fusion.132
  34.9 1.1 copy.10
  36.0 6.6 %all-to-all-start.1 = ((bf16[8,192,256]{2,1,0:T(8,128)(2,1)}), bf16[8,192,256]{2,1,0:T(8,128)(2,1)}, u32[]{:S(2)}, u32[]{:S(2)}) async-start(bf16[8,192,256]{2,1,0:T(8,128)(2,1)} %bitcast.9), calls=%async_computation.1 | async-start | bytes 1572864 | tf_op jit(solution)/shard_map/all_to_all | solution.py:73
  42.6 1.3 slice_bitcast_fusion
  43.9 18.7 %all-to-all-done.1 = bf16[8,192,256]{2,1,0:T(8,128)(2,1)} async-done(((bf16[8,192,256]{2,1,0:T(8,128)(2,1)}), bf16[8,192,256]{2,1,0:T(8,128)(2,1)}, u32[]{:S(2)}, u32[]{:S(2)}) %all-to-all-start.1) | async-done | bytes 786464 | tf_op jit(solution)/shard_map/all_to_all | solution.py:73
  62.6 4.9 %broadcast_add_fusion.1 = f32[8,192,1024]{2,1,0:T(8,128)} fusion(f32[1024]{0:T(1024)S(1)} %bitcast.201, bf16[8,192,256]{2,1,0:T(8,128)(2,1)} %all-to-all-done.1, bf16[2,256,1024]{2,1,0:T(8,128)(2,1)} %param.23), kind=kOutput, calls=%fused_computation.181 | convolution fusion | flops 806879232 | bytes 7606272 | tf_op jit(solution)/shard_map/dot_general | solution.py:9
  67.6 0.9 broadcast.37.clone
  68.5 14.7 %while.30 = (s32[]{:T(128)}, bf16[192,256]{1,0:T(8,128)(2,1)S(1)}, f32[192,256]{1,0:T(8,128)S(1)}, bf16[2,4,192,256]{3,2,1,0:T(8,128)(2,1)}, f32[2,4,192,1024]{3...) while((s32[]{:T(128)}, bf16[192,256]{1,0:T(8,128)(2,1)S(1)}, ...), condition=%wide.region_1.4_spmd.clone, body=%wide.region_0.3_spmd.clone.sunk | while | flops 407863296 | bytes 14680760 | solution.py:27
  68.5 1.4 convolution_add_fusion.16
  69.9 0.2 fusion.215
  70.1 1.4 convolution_add_fusion.17
  71.5 0.2 fusion.216
  71.8 1.4 convolution_add_fusion.18
  73.2 0.2 fusion.217
  73.4 1.4 convolution_add_fusion.19
  74.8 0.2 fusion.218
  75.1 0.8 fusion.219
  75.8 1.4 convolution_add_fusion.16
  77.2 0.2 fusion.215
  77.5 1.4 convolution_add_fusion.17
  78.9 0.2 fusion.216
  79.1 1.4 convolution_add_fusion.18
  80.5 0.2 fusion.217
  80.8 1.4 convolution_add_fusion.19
  82.2 0.2 fusion.218
  82.4 0.8 fusion.219
  83.2 23.8 %all_to_all.30 = bf16[8,192,256]{2,1,0:T(8,128)(2,1)S(1)} all-to-all(bf16[8,192,256]{2,1,0:T(8,128)(2,1)} %bitcast.197), channel_id=1, replica_groups=mesh['tm'=8,'slab'=4] {'tm'}, dimensions={0} | all-to-all | bytes 1572864 | tf_op jit(solution)/shard_map/all_to_all | solution.py:70
  107.0 0.6 gather_fusion.2
  107.8 16.9 %all_to_all.31 = bf16[4,4,128,256]{3,2,1,0:T(8,128)(2,1)S(1)} all-to-all(bf16[4,4,128,256]{3,2,1,0:T(8,128)(2,1)S(1)} %bitcast.195), channel_id=1, replica_groups=mesh['tm'=8,'slab'=4] {'slab'}, dimensions={0} | all-to-all | bytes 2097152 | tf_op jit(solution)/shard_map/all_to_all | solution.py:57
  124.6 2.0 gather_fusion.3
  126.6 3.8 %fusion.126 = bf16[32,256,128]{2,1,0:T(8,128)(2,1)} fusion(bf16[32,128,256]{2,1,0:T(8,128)(2,1)} %gather_fusion.3, pred[32]{0:T(512)(128)(4,1)S(1)} %compare_and_fusion, bf16[1,32,128,128]{3,2,1,0:T(8,128)(2,1)S(1)} %copy-done), kind=kOutput, calls=%fused_computation.182 | convolution fusion | flops 269484032 | bytes 5242912 | tf_op jit(solution)/shard_map/kij,kjf->kif/dot_general | solution.py:60
  130.4 4.5 %copy.13 = bf16[32,256,128]{1,0,2:T(8,128)(2,1)} copy(bf16[32,256,128]{2,1,0:T(8,128)(2,1)} %fusion.126) | data formatting | bytes 4194304 | tf_op jit(solution)/shard_map/kij,kjf->kif/dot_general | solution.py:60
  134.9 2.0 fusion.135
  136.9 1.1 copy.11
  138.0 3.6 %all-to-all-start.4 = ((bf16[8,192,256]{2,1,0:T(8,128)(2,1)}), bf16[8,192,256]{2,1,0:T(8,128)(2,1)S(1)}, u32[]{:S(2)}, u32[]{:S(2)}) async-start(bf16[8,192,256]{2,1,0:T(8,128)(2,1)} %bitcast.20), calls=%async_computation.4 | async-start | bytes 1572864 | tf_op jit(solution)/shard_map/all_to_all | solution.py:73
  141.7 20.0 %all-to-all-done.4 = bf16[8,192,256]{2,1,0:T(8,128)(2,1)S(1)} async-done(((bf16[8,192,256]{2,1,0:T(8,128)(2,1)}), bf16[8,192,256]{2,1,0:T(8,128)(2,1)S(1)}, u32[]{:S(2)}, u32[]{:S(2)}) %all-to-all-start.4) | async-done | bytes 786464 | tf_op jit(solution)/shard_map/all_to_all | solution.py:73
  161.7 4.7 %broadcast_add_fusion = f32[8,192,1024]{2,1,0:T(8,128)} fusion(f32[1024]{0:T(1024)S(1)} %bitcast.200, bf16[8,192,256]{2,1,0:T(8,128)(2,1)S(1)} %all-to-all-done.4, bf16[2,256,1024]{2,1,0:T(8,128)(2,1)} %param.23), kind=kOutput, calls=%fused_computation.180 | convolution fusion | flops 806879232 | bytes 7606272 | tf_op jit(solution)/shard_map/dot_general | solution.py:9
  166.4 13.3 %while.31 = (s32[]{:T(128)}, bf16[192,256]{1,0:T(8,128)(2,1)S(1)}, f32[192,256]{1,0:T(8,128)S(1)}, bf16[2,4,192,256]{3,2,1,0:T(8,128)(2,1)S(1)}, f32[2,4,192,102...) while((s32[]{:T(128)}, bf16[192,256]{1,0:T(8,128)(2,1)S(1)}, ...), condition=%wide.region_3.6_spmd.clone, body=%wide.region_2.5_spmd.clone.sunk | while | flops 407863296 | bytes 14680252 | solution.py:27
  166.4 1.4 convolution_add_fusion.20
  167.9 0.2 fusion.228
  168.1 1.4 convolution_add_fusion.21
  169.5 0.2 fusion.229
  169.7 1.4 convolution_add_fusion.22
  171.1 0.2 fusion.230
  171.4 1.4 convolution_add_fusion.23
  172.8 0.2 fusion.231
  173.1 1.4 convolution_add_fusion.20
  174.5 0.2 fusion.228
  174.7 1.4 convolution_add_fusion.21
  176.1 0.2 fusion.229
  176.4 1.4 convolution_add_fusion.22
  177.8 0.2 fusion.230
  178.0 1.4 convolution_add_fusion.23
  179.4 0.2 fusion.231
  179.7 23.6 %all_to_all.32 = bf16[8,192,256]{2,1,0:T(8,128)(2,1)S(1)} all-to-all(bf16[8,192,256]{2,1,0:T(8,128)(2,1)S(1)} %bitcast.196), channel_id=1, replica_groups=mesh['tm'=8,'slab'=4] {'tm'}, dimensions={0} | all-to-all | bytes 1572864 | tf_op jit(solution)/shard_map/all_to_all | solution.py:70
  203.3 0.9 copy.42
  (25 shorter events, 0.4 us)
Async XLA Ops:
  0.0 24.5 %copy-start = (bf16[1,32,128,128]{3,2,1,0:T(8,128)(2,1)S(1)}, bf16[1,32,128,128]{3,2,1,0:T(8,128)(2,1)}, u32[]{:S(2)}) copy-start(bf16[1,32,128,128]{3,2,1,0:T(8,128)(2,1)} %param.22) | copy-start | bytes 3145732
  2.7 6.1 %copy-start.3 = (s32[1,32]{1,0:T(1,128)S(1)}, s32[1,32]{1,0:T(1,128)}, u32[]{:S(2)}) copy-start(s32[1,32]{1,0:T(1,128)} %param.20) | copy-start | bytes 388
  3.9 18.7 %all-to-all-start = ((bf16[4,4,128,256]{3,2,1,0:T(8,128)(2,1)}), bf16[4,4,128,256]{3,2,1,0:T(8,128)(2,1)S(1)}, u32[]{:S(2)}, u32[]{:S(2)}) async-start(bf16[4,4,128,256]{3,2,1,0:T(8,128)(2,1)} %bitcast.194), calls=%async_computation | async-start | bytes 2097152 | tf_op jit(solution)/shard_map/all_to_all | solution.py:57
  28.3 4.6 %copy-start.2 = (s32[1,32]{1,0:T(1,128)S(1)}, s32[1,32]{1,0:T(1,128)}, u32[]{:S(2)}) copy-start(s32[1,32]{1,0:T(1,128)} %param.19) | copy-start | bytes 388
  34.9 7.7 %copy-start.1 = (f32[2,1024]{1,0:T(2,128)S(1)}, f32[2,1024]{1,0:T(2,128)}, u32[]{:S(2)}) copy-start(f32[2,1024]{1,0:T(2,128)} %param.25) | copy-start | bytes 24580
  36.0 26.6 %all-to-all-start.1 = ((bf16[8,192,256]{2,1,0:T(8,128)(2,1)}), bf16[8,192,256]{2,1,0:T(8,128)(2,1)}, u32[]{:S(2)}, u32[]{:S(2)}) async-start(bf16[8,192,256]{2,1,0:T(8,128)(2,1)} %bitcast.9), calls=%async_computation.1 | async-start | bytes 1572864 | tf_op jit(solution)/shard_map/all_to_all | solution.py:73
  138.0 23.6 %all-to-all-start.4 = ((bf16[8,192,256]{2,1,0:T(8,128)(2,1)}), bf16[8,192,256]{2,1,0:T(8,128)(2,1)S(1)}, u32[]{:S(2)}, u32[]{:S(2)}) async-start(bf16[8,192,256]{2,1,0:T(8,128)(2,1)} %bitcast.20), calls=%async_computation.4 | async-start | bytes 1572864 | tf_op jit(solution)/shard_map/all_to_all | solution.py:73
where the time goes:
time: 206 us; the launch traced here: 204 us
  blocking collectives  64.2 us (31%)
  waiting for transfers between devices  52.5 us (25%)
  matrix products  43.7 us (21%)
  local copies, waits for them, and re-layouts  21.8 us (11%)
  starting transfers between devices  14.4 us (7%)
  other arithmetic  6.52 us (3%)
    all_to_all x2, blocking collectives, recur(): return lax.all_to_all(states, 'tm', split_axis=0, concat_axis=0, tiled=True)  47.3 us
    all_to_all x2, waiting for transfers between devices, local(): lax.all_to_all(grouped, 'tm', split_axis=0, concat_axis=0, tiled=True)  38.7 us
    dot_general x16, matrix products, advance(): jnp.dot(hidden, weight_rec, preferred_element_type=jnp.float32)  22.5 us
    all_to_all x1, blocking collectives, local(): lax.all_to_all(outgoing, 'slab', split_axis=0, concat_axis=0, tiled=True)  16.9 us
    all_to_all x1, waiting for transfers between devices, local(): lax.all_to_all(outgoing, 'slab', split_axis=0, concat_axis=0, tiled=True)  13.7 us
    all_to_all x2, starting transfers between devices, local(): lax.all_to_all(grouped, 'tm', split_axis=0, concat_axis=0, tiled=True)  10.2 us
    dot_general x2, matrix products, lstm_run(): jnp.dot(inputs.reshape(-1, feature_width), weight_in, preferred_element_t...  9.61 us
    dot_general x2, local copies, waits for them, and re-layouts, local(): jnp.einsum('kij,kjf->kif', weight_tiles, picked, preferred_element_type=j...  9.1 us
  transfers between devices with their start and end apart: 3, of which 3 were waited for; matrix products, arithmetic and copies ran while one was open for 1% of the time, Pallas kernels for 0%

commit v1 on v0

v1 whole, which is shorter than its diff:
```python
import jax
import jax.numpy as jnp
from jax import lax
from jax.experimental import pallas as pl
from jax.experimental.pallas import tpu as pltpu
from jax.sharding import PartitionSpec as P


ANY = pl.BlockSpec(memory_space=pl.ANY)
SMEM = pl.BlockSpec(memory_space=pltpu.SMEM)
VMEM = pl.BlockSpec(memory_space=pltpu.VMEM)
PARAMS = pltpu.CompilerParams(vmem_limit_bytes=24 * 2**20)
UNROLL = 4
AXES = ("tm", "slab")
LOWER, UPPER, BOTH = 0, 1, None


def seat(group):
    index = lax.axis_index("tm")
    half = index // group
    place = index % group
    return half, place, place ^ (half * mirror(group))


def mirror(group):
    return group - 2 if group > 2 else 0


def only(mode, half):
    def run(body):
        if mode is BOTH:
            body()
        else:
            pl.when(half == mode)(body)

    return run


def pick_tiles(parts, ref_table, slab_count, row_count, tile, group, mode):
    part_count = len(parts)
    part_rows, width = parts[0].shape
    listed = ref_table.shape[2] // slab_count

    def kernel(table, *refs):
        sources = refs[:part_count]
        outs = refs[part_count : part_count + slab_count]
        slab = lax.axis_index("slab")
        half, _, lead = seat(group)

        @only(mode, half)
        def _():
            rows = sources[0]
            if part_count > 1:
                rows = refs[-1]
                for k in range(part_count):
                    start = pl.multiple_of((lead ^ k) * part_rows, part_rows)
                    rows[pl.ds(start, part_rows), :] = sources[k][...]
            for k in reversed(range(slab_count)):
                for j in range(listed):
                    index = table[0, slab ^ k, slab * listed + j]
                    start = pl.multiple_of(index * tile, tile)
                    outs[k][j * tile : (j + 1) * tile, :] = rows[pl.ds(start, tile), :]

    dtype = parts[0].dtype
    return pl.pallas_call(
        kernel,
        in_specs=[SMEM] + [VMEM] * part_count,
        out_specs=[VMEM] * slab_count,
        out_shape=[jax.ShapeDtypeStruct((listed * tile, width), dtype)] * slab_count,
        scratch_shapes=[pltpu.VMEM((row_count, width), dtype)] if part_count > 1 else [],
        compiler_params=PARAMS,
        name="pick_tiles",
    )(ref_table, *parts)


def convolve(arrived, tile_rows, tile_sources, tile_counts, tile_values, row_count, group, mode):
    slab_count = len(arrived)
    piece, width = arrived[0].shape
    tile = tile_values.shape[2]
    group_rows = row_count // group

    def kernel(rows, sources, counts, values, *refs):
        pieces = refs[:slab_count]
        outs = refs[slab_count : slab_count + group]
        inputs, total = refs[slab_count + group :]
        slab = lax.axis_index("slab")
        half, _, lead = seat(group)

        @only(mode, half)
        def _():
            for k in range(slab_count):
                start = pl.multiple_of((slab ^ k) * piece, piece)
                inputs[pl.ds(start, piece), :] = pieces[k][...]
            total[...] = jnp.zeros_like(total)
            count = counts[0, 0]

            def step(index, carry):
                products = []
                for lane in range(UNROLL):
                    slot = index * UNROLL + lane
                    start = pl.multiple_of(sources[0, slot] * tile, tile)
                    product = jnp.dot(
                        values[0, slot],
                        inputs[pl.ds(start, tile), :],
                        preferred_element_type=jnp.float32,
                    )
                    products.append(jnp.where(slot < count, product, 0.0))
                for lane in range(UNROLL):
                    target = pl.multiple_of(rows[0, index * UNROLL + lane] * tile, tile)
                    total[pl.ds(target, tile), :] += products[lane]
                return carry

            lax.fori_loop(0, (count + UNROLL - 1) // UNROLL, step, 0)
            for k in range(group):
                start = pl.multiple_of((lead ^ k) * group_rows, group_rows)
                outs[k][...] = total[pl.ds(start, group_rows), :].astype(outs[k].dtype)

    dtype = arrived[0].dtype
    return pl.pallas_call(
        kernel,
        in_specs=[SMEM, SMEM, SMEM, VMEM] + [VMEM] * slab_count,
        out_specs=[VMEM] * group,
        out_shape=[jax.ShapeDtypeStruct((group_rows, width), dtype)] * group,
        scratch_shapes=[
            pltpu.VMEM((slab_count * piece, width), dtype),
            pltpu.VMEM((row_count, width), jnp.float32),
        ],
        compiler_params=PARAMS,
        name="convolve",
    )(tile_rows, tile_sources, tile_counts, tile_values, *arrived)


def sigmoid(value):
    return 0.5 * jnp.tanh(0.5 * value) + 0.5


def recur(mixed, layer, w_input, w_hidden, bias, mode, state=None, after=None):
    group = len(mixed)
    rows, width = mixed[0].shape
    units = w_hidden.shape[1]
    extra = [value for value in (state, after) if value is not None]
    first = group + len(extra)

    def kernel(w_in, w_rec, gate_bias, *refs):
        sources = refs[:group]
        outs = refs[first : first + group]
        last, token = refs[first + group : first + group + 2]
        inputs, states, memory = refs[first + group + 2 :]
        half, place, _ = seat(group)

        @only(mode, half)
        def _():
            for k in range(group):
                inputs[place ^ k] = sources[k][...]
            line = gate_bias[layer : layer + 1, :]

            def advance(gates, old, time):
                i, f, g, o = (gates[:, n * units : (n + 1) * units] for n in range(4))
                new = sigmoid(i) * jnp.tanh(g)
                if old is not None:
                    new = sigmoid(f) * old + new
                memory[...] = new
                states[time] = (sigmoid(o) * jnp.tanh(new)).astype(states.dtype)

            def project(time):
                return jnp.dot(inputs[time], w_in[layer], preferred_element_type=jnp.float32) + line

            def step(time, carry):
                gates = project(time) + jnp.dot(
                    carry, w_rec[layer], preferred_element_type=jnp.float32
                )
                advance(gates, memory[...], time)
                return states[time]

            if state is None:
                advance(project(0), None, 0)
            else:
                memory[...] = refs[group][1].astype(jnp.float32)
                step(0, refs[group][0])

            def loop(time, carry):
                step(time, states[time - 1])
                return carry

            lax.fori_loop(1, group, loop, 0)
            for k in range(group):
                outs[k][...] = states[place ^ k]
            last[0] = states[group - 1]
            last[1] = memory[...].astype(last.dtype)

        token[...] = jnp.zeros_like(token)

    dtype = mixed[0].dtype
    *hidden, last, token = pl.pallas_call(
        kernel,
        in_specs=[VMEM] * (3 + first),
        out_specs=[VMEM] * (group + 2),
        out_shape=[jax.ShapeDtypeStruct((rows, units), dtype)] * group
        + [
            jax.ShapeDtypeStruct((2, rows, units), dtype),
            jax.ShapeDtypeStruct((8, 128), jnp.float32),
        ],
        scratch_shapes=[
            pltpu.VMEM((group, rows, width), dtype),
            pltpu.VMEM((group, rows, units), dtype),
            pltpu.VMEM((rows, units), jnp.float32),
        ],
        compiler_params=PARAMS,
        name="recur",
    )(w_input, w_hidden, bias, *mixed, *extra)
    return hidden, last, token


def assemble(lists, group):
    part_rows, width = lists[0][0].shape

    def kernel(*refs):
        out, sems = refs[-2:]
        half, _, lead = seat(group)
        for mode in range(len(lists)):

            @only(mode, half)
            def _():
                copies = []
                for k in range(group):
                    start = pl.multiple_of((lead ^ k) * part_rows, part_rows)
                    copies.append(
                        pltpu.make_async_copy(
                            refs[mode * group + k], out.at[0, pl.ds(start, part_rows)], sems.at[k]
                        )
                    )
                for copy in copies:
                    copy.start()
                for copy in copies:
                    copy.wait()

    parts = [part for parts in lists for part in parts]
    return pl.pallas_call(
        kernel,
        in_specs=[VMEM] * len(parts),
        out_specs=ANY,
        out_shape=jax.ShapeDtypeStruct((1, group * part_rows, width), parts[0].dtype),
        scratch_shapes=[pltpu.SemaphoreType.DMA((group,))],
        compiler_params=PARAMS,
        name="assemble",
    )(*parts)


def send(array, group, mode, target):
    slab_count = lax.axis_size("slab")
    pairs = []
    for time in range(lax.axis_size("tm")):
        if mode is BOTH or time // group == mode:
            for slab in range(slab_count):
                to_time, to_slab = target(time, slab)
                pairs.append((time * slab_count + slab, to_time * slab_count + to_slab))
    return lax.ppermute(array, AXES, pairs)


def swap_slabs(arrays, group, mode):
    got = list(arrays)
    for k in range(len(arrays) - 1, 0, -1):
        got[k] = send(arrays[k], group, mode, lambda time, slab: (time, slab ^ k))
    return got


def swap_times(arrays, group, mode):
    got = list(arrays)
    for k in range(len(arrays) - 1, 0, -1):
        got[k] = send(arrays[k], group, mode, lambda time, slab: (time ^ k, slab))
    return got


def hand_over(last, group):
    return send(
        last, group, LOWER, lambda time, slab: (group + (time ^ mirror(group)), slab)
    )


def local(
    features, ref_lists, tile_rows, tile_sources, tile_counts, tile_values, w_input, w_hidden, bias
):
    row_count = features.shape[1]
    tile = tile_values.shape[2]
    slab_count = lax.axis_size("slab")
    layers = w_input.shape[0]
    group = lax.axis_size("tm") // 2

    def mix(parts, mode):
        listed = pick_tiles(parts, ref_lists, slab_count, row_count, tile, group, mode)
        arrived = swap_slabs(listed, group, mode)
        mixed = convolve(
            arrived, tile_rows, tile_sources, tile_counts, tile_values, row_count, group, mode
        )
        return swap_times(mixed, group, mode)

    def run(mixed, layer, mode, state=None, after=None):
        return recur(mixed, layer, w_input, w_hidden, bias, mode, state, after)

    mixed = mix([features[0]], BOTH)
    lower_mixed, upper_mixed = mixed, mixed
    handed, token = [], None
    for layer in range(layers + 1):
        if layer < layers:
            hidden, last, token = run(lower_mixed, layer, LOWER)
            handed.append(hand_over(last, group))
            lower = swap_times(hidden, group, LOWER)
            if layer + 1 < layers:
                lower_mixed = mix(lower, LOWER)
        if layer > 0:
            hidden, _, _ = run(upper_mixed, layer - 1, UPPER, handed[layer - 1], token)
            upper = swap_times(hidden, group, UPPER)
            if layer < layers:
                upper_mixed = mix(upper, UPPER)
    return assemble([lower, upper], group)


def solution(mesh):
    in_specs = (
        P("tm", "slab", None),
        P("tm", None, None),
        P("tm", "slab"),
        P("tm", "slab"),
        P("tm", "slab"),
        P("tm", "slab", None, None),
        P(),
        P(),
        P(),
    )
    out_specs = P("tm", "slab", None)
    return jax.shard_map(local, mesh=mesh, in_specs=in_specs, out_specs=out_specs, check_vma=False)
```

time: 206 us -> 157 us (0.76)
  the two profiles are of different devices: /device:TPU:0 before, /device:TPU:18 now
where the time goes in v1:
time: 157 us; the launch traced here: 156 us
  waiting for transfers between devices  84.4 us (54%)
  starting transfers between devices  51.3 us (33%)
  Pallas kernels  16.1 us (10%)
  local copies, waits for them, and re-layouts  3.08 us (2%)
    ppermute x32, waiting for transfers between devices, send(): return lax.ppermute(array, AXES, pairs)  84.4 us
    ppermute x32, starting transfers between devices, send(): return lax.ppermute(array, AXES, pairs)  51.3 us
    pallas_call x4, Pallas kernels, recur(): pl.pallas_call(kernel, in_specs=[VMEM] * (3 + first), out_specs=[VMEM] *...  7.85 us
    pallas_call x3, Pallas kernels, convolve(): pl.pallas_call(kernel, in_specs=[SMEM, SMEM, SMEM, VMEM] + [VMEM] * slab_...  5.38 us
  transfers between devices with their start and end apart: 32, of which 14 were waited for; matrix products, arithmetic and copies ran while one was open for 0% of the time, Pallas kernels for 4%

profile of v1, /device:TPU:18, one launch (start us, length us, event | category | flops | bytes accessed | tf_op | source)
XLA Modules:
  0.0 156.0 jit_solution(15894436647077005977)
XLA Ops:
  0.0 1.1 copy-done.4
  1.1 0.7 copy-done.6
  1.8 0.6 pick_tiles.3
  2.5 0.1 collective-permute-start
  2.5 0.6 collective-permute-start.1
  3.1 1.2 collective-permute-start.2
  5.0 0.0 copy-start.8
  5.1 0.0 copy-start.9
  5.1 0.0 collective-permute-done.refs_1_
  5.1 6.7 %collective-permute-done.1.refs_2_ = bf16[512,256]{1,0:T(8,128)(2,1)S(1)} collective-permute-done((bf16[512,256]{1,0:T(8,128)(2,1)S(1)}, bf16[512,256]{1,0:T(8,128)(2,1)S(1)}, u32[]{:S(2)}, u32[]{:S(2)}) %collective-permute-start.1) | collective-permute-done | bytes 262176 | tf_op jit(solution)/shard_map/ppermute | solution.py:257
  11.8 4.5 %collective-permute-done.2.refs_3_ = bf16[512,256]{1,0:T(8,128)(2,1)S(1)} collective-permute-done((bf16[512,256]{1,0:T(8,128)(2,1)S(1)}, bf16[512,256]{1,0:T(8,128)(2,1)S(1)}, u32[]{:S(2)}, u32[]{:S(2)}) %collective-permute-start.2) | collective-permute-done | bytes 262176 | tf_op jit(solution)/shard_map/ppermute | solution.py:257
  16.3 1.2 copy-done.2
  17.6 2.4 %convolve.3 = (bf16[384,256]{1,0:T(8,128)(2,1)S(1)}, bf16[384,256]{1,0:T(8,128)(2,1)S(1)}, bf16[384,256]{1,0:T(8,128)(2,1)S(1)}, bf16[384,256]{1,0:T(8,128)(2,1)S(1)}) custom-call(s32[1,32]{1,0:T(1,128)S(1)} %copy-done.8, s32[1,32]{1,0:T(1,128)S(1)} %copy-done.9, s32[1,1]{1,0:T(1,128)S(6)} %copy.10.counts, bf16[1,32,128,128]{3,2,1,0:T(8,128)(2,1)S(1)} %copy-done.2, ...), custom_call_target="tpu_custom_call" | custom-call | tf_op jit(solution)/shard_map/convolve/pallas_call | solution.py:119
  20.0 1.8 %collective-permute-start.3 = (bf16[384,256]{1,0:T(8,128)(2,1)S(1)}, bf16[384,256]{1,0:T(8,128)(2,1)S(1)}, u32[]{:S(2)}, u32[]{:S(2)}) collective-permute-start(bf16[384,256]{1,0:T(8,128)(2,1)S(1)} %get-tuple-element.53), channel_id=1, source_target_pairs={{0,4},{1,5},{2,6},{3,7},{4,0},{5,1},{6,2},{7,3},{8,12},{9,13},{10,... | collective-permute-start | bytes 589832 | tf_op jit(solution)/shard_map/ppermute | solution.py:257
  21.8 1.3 collective-permute-start.4
  23.1 0.4 collective-permute-start.5
  23.5 3.7 %collective-permute-done.3.refs_1_ = bf16[384,256]{1,0:T(8,128)(2,1)S(1)} collective-permute-done((bf16[384,256]{1,0:T(8,128)(2,1)S(1)}, bf16[384,256]{1,0:T(8,128)(2,1)S(1)}, u32[]{:S(2)}, u32[]{:S(2)}) %collective-permute-start.3) | collective-permute-done | bytes 196640 | tf_op jit(solution)/shard_map/ppermute | solution.py:257
  27.2 2.3 %collective-permute-done.4.refs_2_ = bf16[384,256]{1,0:T(8,128)(2,1)S(1)} collective-permute-done((bf16[384,256]{1,0:T(8,128)(2,1)S(1)}, bf16[384,256]{1,0:T(8,128)(2,1)S(1)}, u32[]{:S(2)}, u32[]{:S(2)}) %collective-permute-start.4) | collective-permute-done | bytes 196640 | tf_op jit(solution)/shard_map/ppermute | solution.py:257
  29.6 3.1 %collective-permute-done.5.refs_3_ = bf16[384,256]{1,0:T(8,128)(2,1)S(1)} collective-permute-done((bf16[384,256]{1,0:T(8,128)(2,1)S(1)}, bf16[384,256]{1,0:T(8,128)(2,1)S(1)}, u32[]{:S(2)}, u32[]{:S(2)}) %collective-permute-start.5) | collective-permute-done | bytes 196640 | tf_op jit(solution)/shard_map/ppermute | solution.py:257
  32.7 0.0 copy-start.3
  32.7 0.6 recur.4
  33.3 0.7 collective-permute-start.6
  34.0 0.0 copy-start.7
  34.0 0.7 collective-permute-start.7
  34.7 0.7 collective-permute-start.8
  35.4 0.6 pick_tiles.4
  36.0 0.7 collective-permute-start.9
  36.7 0.7 collective-permute-start.10
  37.4 0.7 collective-permute-start.11
  38.1 1.3 collective-permute-start.18
  39.4 0.6 convolve.4
  40.0 0.7 collective-permute-start.12
  40.7 0.7 collective-permute-start.13
  41.4 0.7 collective-permute-start.14
  42.1 36.8 %collective-permute-done.18.refs_4_ = bf16[2,384,256]{2,1,0:T(8,128)(2,1)S(1)} collective-permute-done((bf16[2,384,256]{2,1,0:T(8,128)(2,1)S(1)}, bf16[2,384,256]{2,1,0:T(8,128)(2,1)S(1)}, u32[]{:S(2)}, u32[]{:S(2)}) %collective-permute-start.18) | collective-permute-done | bytes 393248 | tf_op jit(solution)/shard_map/ppermute | solution.py:257
  78.9 3.6 %recur.6 = (bf16[384,256]{1,0:T(8,128)(2,1)S(1)}, bf16[384,256]{1,0:T(8,128)(2,1)S(1)}, bf16[384,256]{1,0:T(8,128)(2,1)S(1)}, bf16[384,256]{1,0:T(8,128)(2,1)S(1...) custom-call(bf16[2,256,1024]{2,1,0:T(8,128)(2,1)S(1)} %copy-done, bf16[2,256,1024]{2,1,0:T(8,128)(2,1)S(1)} %copy-done.1, ...), custom_call_target="tpu_custom_call" | custom-call | tf_op jit(solution)/shard_map/recur/pallas_call | solution.py:194
  82.5 3.6 %collective-permute-start.19 = (bf16[384,256]{1,0:T(8,128)(2,1)S(1)}, bf16[384,256]{1,0:T(8,128)(2,1)S(1)}, u32[]{:S(2)}, u32[]{:S(2)}) collective-permute-start(bf16[384,256]{1,0:T(8,128)(2,1)S(1)} %get-tuple-element.75), channel_id=1, source_target_pairs={{16,20},{17,21},{18,22},{19,23},{20,16},{21,17},{22,18},{23,19},{2... | collective-permute-start | bytes 589832 | tf_op jit(solution)/shard_map/ppermute | solution.py:257
  86.1 1.9 %collective-permute-start.20 = (bf16[384,256]{1,0:T(8,128)(2,1)S(1)}, bf16[384,256]{1,0:T(8,128)(2,1)S(1)}, u32[]{:S(2)}, u32[]{:S(2)}) collective-permute-start(bf16[384,256]{1,0:T(8,128)(2,1)S(1)} %get-tuple-element.76), channel_id=1, source_target_pairs={{16,24},{17,25},{18,26},{19,27},{20,28},{21,29},{22,30},{23,31},{2... | collective-permute-start | bytes 589832 | tf_op jit(solution)/shard_map/ppermute | solution.py:257
  88.0 3.6 %collective-permute-start.21 = (bf16[384,256]{1,0:T(8,128)(2,1)S(1)}, bf16[384,256]{1,0:T(8,128)(2,1)S(1)}, u32[]{:S(2)}, u32[]{:S(2)}) collective-permute-start(bf16[384,256]{1,0:T(8,128)(2,1)S(1)} %get-tuple-element.77), channel_id=1, source_target_pairs={{16,28},{17,29},{18,30},{19,31},{20,24},{21,25},{22,26},{23,27},{2... | collective-permute-start | bytes 589832 | tf_op jit(solution)/shard_map/ppermute | solution.py:257
  91.7 4.1 %collective-permute-done.20.refs_2_ = bf16[384,256]{1,0:T(8,128)(2,1)S(1)} collective-permute-done((bf16[384,256]{1,0:T(8,128)(2,1)S(1)}, bf16[384,256]{1,0:T(8,128)(2,1)S(1)}, u32[]{:S(2)}, u32[]{:S(2)}) %collective-permute-start.20) | collective-permute-done | bytes 196640 | tf_op jit(solution)/shard_map/ppermute | solution.py:257
  95.8 2.4 %collective-permute-done.21.refs_3_ = bf16[384,256]{1,0:T(8,128)(2,1)S(1)} collective-permute-done((bf16[384,256]{1,0:T(8,128)(2,1)S(1)}, bf16[384,256]{1,0:T(8,128)(2,1)S(1)}, u32[]{:S(2)}, u32[]{:S(2)}) %collective-permute-start.21) | collective-permute-done | bytes 196640 | tf_op jit(solution)/shard_map/ppermute | solution.py:257
  98.2 0.7 pick_tiles.5
  98.9 1.9 %collective-permute-start.22 = (bf16[512,256]{1,0:T(8,128)(2,1)S(1)}, bf16[512,256]{1,0:T(8,128)(2,1)S(1)}, u32[]{:S(2)}, u32[]{:S(2)}) collective-permute-start(bf16[512,256]{1,0:T(8,128)(2,1)S(1)} %get-tuple-element.79), channel_id=1, source_target_pairs={{16,17},{17,16},{18,19},{19,18},{20,21},{21,20},{22,23},{23,22},{2... | collective-permute-start | bytes 786440 | tf_op jit(solution)/shard_map/ppermute | solution.py:257
  100.8 2.8 %collective-permute-start.23 = (bf16[512,256]{1,0:T(8,128)(2,1)S(1)}, bf16[512,256]{1,0:T(8,128)(2,1)S(1)}, u32[]{:S(2)}, u32[]{:S(2)}) collective-permute-start(bf16[512,256]{1,0:T(8,128)(2,1)S(1)} %get-tuple-element.80), channel_id=1, source_target_pairs={{16,18},{17,19},{18,16},{19,17},{20,22},{21,23},{22,20},{23,21},{2... | collective-permute-start | bytes 786440 | tf_op jit(solution)/shard_map/ppermute | solution.py:257
  103.7 2.9 %collective-permute-start.24 = (bf16[512,256]{1,0:T(8,128)(2,1)S(1)}, bf16[512,256]{1,0:T(8,128)(2,1)S(1)}, u32[]{:S(2)}, u32[]{:S(2)}) collective-permute-start(bf16[512,256]{1,0:T(8,128)(2,1)S(1)} %get-tuple-element.81), channel_id=1, source_target_pairs={{16,19},{17,18},{18,17},{19,16},{20,23},{21,22},{22,21},{23,20},{2... | collective-permute-start | bytes 786440 | tf_op jit(solution)/shard_map/ppermute | solution.py:257
  106.5 1.3 collective-permute-start.28
  107.8 4.1 %collective-permute-done.23.refs_2_ = bf16[512,256]{1,0:T(8,128)(2,1)S(1)} collective-permute-done((bf16[512,256]{1,0:T(8,128)(2,1)S(1)}, bf16[512,256]{1,0:T(8,128)(2,1)S(1)}, u32[]{:S(2)}, u32[]{:S(2)}) %collective-permute-start.23) | collective-permute-done | bytes 262176 | tf_op jit(solution)/shard_map/ppermute | solution.py:257
  111.9 4.7 %collective-permute-done.24.refs_3_ = bf16[512,256]{1,0:T(8,128)(2,1)S(1)} collective-permute-done((bf16[512,256]{1,0:T(8,128)(2,1)S(1)}, bf16[512,256]{1,0:T(8,128)(2,1)S(1)}, u32[]{:S(2)}, u32[]{:S(2)}) %collective-permute-start.24) | collective-permute-done | bytes 262176 | tf_op jit(solution)/shard_map/ppermute | solution.py:257
  116.6 2.4 %convolve.5 = (bf16[384,256]{1,0:T(8,128)(2,1)S(1)}, bf16[384,256]{1,0:T(8,128)(2,1)S(1)}, bf16[384,256]{1,0:T(8,128)(2,1)S(1)}, bf16[384,256]{1,0:T(8,128)(2,1)S(1)}) custom-call(s32[1,32]{1,0:T(1,128)S(1)} %copy-done.8, s32[1,32]{1,0:T(1,128)S(1)} %copy-done.9, s32[1,1]{1,0:T(1,128)S(6)} %copy.10.counts, bf16[1,32,128,128]{3,2,1,0:T(8,128)(2,1)S(1)} %copy-done.3, ...), custom_call_target="tpu_custom_call" | custom-call | tf_op jit(solution)/shard_map/convolve/pallas_call | solution.py:119
  119.0 3.9 %collective-permute-start.25 = (bf16[384,256]{1,0:T(8,128)(2,1)S(1)}, bf16[384,256]{1,0:T(8,128)(2,1)S(1)}, u32[]{:S(2)}, u32[]{:S(2)}) collective-permute-start(bf16[384,256]{1,0:T(8,128)(2,1)S(1)} %get-tuple-element.83), channel_id=1, source_target_pairs={{16,20},{17,21},{18,22},{19,23},{20,16},{21,17},{22,18},{23,19},{2... | collective-permute-start | bytes 589832 | tf_op jit(solution)/shard_map/ppermute | solution.py:257
  122.9 2.0 %collective-permute-start.26 = (bf16[384,256]{1,0:T(8,128)(2,1)S(1)}, bf16[384,256]{1,0:T(8,128)(2,1)S(1)}, u32[]{:S(2)}, u32[]{:S(2)}) collective-permute-start(bf16[384,256]{1,0:T(8,128)(2,1)S(1)} %get-tuple-element.84), channel_id=1, source_target_pairs={{16,24},{17,25},{18,26},{19,27},{20,28},{21,29},{22,30},{23,31},{2... | collective-permute-start | bytes 589832 | tf_op jit(solution)/shard_map/ppermute | solution.py:257
  124.9 3.4 %collective-permute-start.27 = (bf16[384,256]{1,0:T(8,128)(2,1)S(1)}, bf16[384,256]{1,0:T(8,128)(2,1)S(1)}, u32[]{:S(2)}, u32[]{:S(2)}) collective-permute-start(bf16[384,256]{1,0:T(8,128)(2,1)S(1)} %get-tuple-element.85), channel_id=1, source_target_pairs={{16,28},{17,29},{18,30},{19,31},{20,24},{21,25},{22,26},{23,27},{2... | collective-permute-start | bytes 589832 | tf_op jit(solution)/shard_map/ppermute | solution.py:257
  128.2 0.7 collective-permute-start.15
  128.9 0.7 collective-permute-start.16
  129.6 0.7 collective-permute-start.17
  130.3 2.2 %collective-permute-done.26.refs_2_ = bf16[384,256]{1,0:T(8,128)(2,1)S(1)} collective-permute-done((bf16[384,256]{1,0:T(8,128)(2,1)S(1)}, bf16[384,256]{1,0:T(8,128)(2,1)S(1)}, u32[]{:S(2)}, u32[]{:S(2)}) %collective-permute-start.26) | collective-permute-done | bytes 196640 | tf_op jit(solution)/shard_map/ppermute | solution.py:257
  132.5 3.3 %collective-permute-done.27.refs_3_ = bf16[384,256]{1,0:T(8,128)(2,1)S(1)} collective-permute-done((bf16[384,256]{1,0:T(8,128)(2,1)S(1)}, bf16[384,256]{1,0:T(8,128)(2,1)S(1)}, u32[]{:S(2)}, u32[]{:S(2)}) %collective-permute-start.27) | collective-permute-done | bytes 196640 | tf_op jit(solution)/shard_map/ppermute | solution.py:257
  135.8 3.6 %recur.7 = (bf16[384,256]{1,0:T(8,128)(2,1)S(1)}, bf16[384,256]{1,0:T(8,128)(2,1)S(1)}, bf16[384,256]{1,0:T(8,128)(2,1)S(1)}, bf16[384,256]{1,0:T(8,128)(2,1)S(1...) custom-call(bf16[2,256,1024]{2,1,0:T(8,128)(2,1)S(1)} %copy-done, bf16[2,256,1024]{2,1,0:T(8,128)(2,1)S(1)} %copy-done.1, ...), custom_call_target="tpu_custom_call" | custom-call | tf_op jit(solution)/shard_map/recur/pallas_call | solution.py:194
  139.4 3.6 %collective-permute-start.29 = (bf16[384,256]{1,0:T(8,128)(2,1)S(1)}, bf16[384,256]{1,0:T(8,128)(2,1)S(1)}, u32[]{:S(2)}, u32[]{:S(2)}) collective-permute-start(bf16[384,256]{1,0:T(8,128)(2,1)S(1)} %get-tuple-element.88), channel_id=1, source_target_pairs={{16,20},{17,21},{18,22},{19,23},{20,16},{21,17},{22,18},{23,19},{2... | collective-permute-start | bytes 589832 | tf_op jit(solution)/shard_map/ppermute | solution.py:257
  143.1 2.2 %collective-permute-start.30 = (bf16[384,256]{1,0:T(8,128)(2,1)S(1)}, bf16[384,256]{1,0:T(8,128)(2,1)S(1)}, u32[]{:S(2)}, u32[]{:S(2)}) collective-permute-start(bf16[384,256]{1,0:T(8,128)(2,1)S(1)} %get-tuple-element.89), channel_id=1, source_target_pairs={{16,24},{17,25},{18,26},{19,27},{20,28},{21,29},{22,30},{23,31},{2... | collective-permute-start | bytes 589832 | tf_op jit(solution)/shard_map/ppermute | solution.py:257
  145.3 3.4 %collective-permute-start.31 = (bf16[384,256]{1,0:T(8,128)(2,1)S(1)}, bf16[384,256]{1,0:T(8,128)(2,1)S(1)}, u32[]{:S(2)}, u32[]{:S(2)}) collective-permute-start(bf16[384,256]{1,0:T(8,128)(2,1)S(1)} %get-tuple-element.90), channel_id=1, source_target_pairs={{16,28},{17,29},{18,30},{19,31},{20,24},{21,25},{22,26},{23,27},{2... | collective-permute-start | bytes 589832 | tf_op jit(solution)/shard_map/ppermute | solution.py:257
  148.7 4.0 %collective-permute-done.30.refs_6_ = bf16[384,256]{1,0:T(8,128)(2,1)S(1)} collective-permute-done((bf16[384,256]{1,0:T(8,128)(2,1)S(1)}, bf16[384,256]{1,0:T(8,128)(2,1)S(1)}, u32[]{:S(2)}, u32[]{:S(2)}) %collective-permute-start.30) | collective-permute-done | bytes 196640 | tf_op jit(solution)/shard_map/ppermute | solution.py:257
  152.7 2.4 %collective-permute-done.31.refs_7_ = bf16[384,256]{1,0:T(8,128)(2,1)S(1)} collective-permute-done((bf16[384,256]{1,0:T(8,128)(2,1)S(1)}, bf16[384,256]{1,0:T(8,128)(2,1)S(1)}, u32[]{:S(2)}, u32[]{:S(2)}) %collective-permute-start.31) | collective-permute-done | bytes 196640 | tf_op jit(solution)/shard_map/ppermute | solution.py:257
  155.1 0.9 assemble.1
  (31 shorter events, 0.1 us)
Async XLA Ops:
  0.0 1.1 copy-start.4
  1.1 0.7 copy-start.6
  2.5 2.6 %collective-permute-start = (bf16[512,256]{1,0:T(8,128)(2,1)S(1)}, bf16[512,256]{1,0:T(8,128)(2,1)S(1)}, u32[]{:S(2)}, u32[]{:S(2)}) collective-permute-start(bf16[512,256]{1,0:T(8,128)(2,1)S(1)} %get-tuple-element.49), channel_id=1, source_target_pairs={{0,1},{1,0},{2,3},{3,2},{4,5},{5,4},{6,7},{7,6},{8,9},{9,8},{10,11... | collective-permute-start | bytes 786440 | tf_op jit(solution)/shard_map/ppermute | solution.py:257
  2.5 9.2 %collective-permute-start.1 = (bf16[512,256]{1,0:T(8,128)(2,1)S(1)}, bf16[512,256]{1,0:T(8,128)(2,1)S(1)}, u32[]{:S(2)}, u32[]{:S(2)}) collective-permute-start(bf16[512,256]{1,0:T(8,128)(2,1)S(1)} %get-tuple-element.50), channel_id=1, source_target_pairs={{0,2},{1,3},{2,0},{3,1},{4,6},{5,7},{6,4},{7,5},{8,10},{9,11},{10,... | collective-permute-start | bytes 786440 | tf_op jit(solution)/shard_map/ppermute | solution.py:257
  3.1 13.2 %collective-permute-start.2 = (bf16[512,256]{1,0:T(8,128)(2,1)S(1)}, bf16[512,256]{1,0:T(8,128)(2,1)S(1)}, u32[]{:S(2)}, u32[]{:S(2)}) collective-permute-start(bf16[512,256]{1,0:T(8,128)(2,1)S(1)} %get-tuple-element.51), channel_id=1, source_target_pairs={{0,3},{1,2},{2,1},{3,0},{4,7},{5,6},{6,5},{7,4},{8,11},{9,10},{10,... | collective-permute-start | bytes 786440 | tf_op jit(solution)/shard_map/ppermute | solution.py:257
  5.0 11.3 %copy-start.8 = (s32[1,32]{1,0:T(1,128)S(1)}, s32[1,32]{1,0:T(1,128)}, u32[]{:S(2)}) copy-start(s32[1,32]{1,0:T(1,128)} %rows.5) | copy-start | bytes 388
  5.1 11.3 %copy-start.9 = (s32[1,32]{1,0:T(1,128)S(1)}, s32[1,32]{1,0:T(1,128)}, u32[]{:S(2)}) copy-start(s32[1,32]{1,0:T(1,128)} %sources.5) | copy-start | bytes 388
  16.3 1.2 copy-start.2
  17.6 15.1 %copy-start = (bf16[2,256,1024]{2,1,0:T(8,128)(2,1)S(1)}, bf16[2,256,1024]{2,1,0:T(8,128)(2,1)}, u32[]{:S(2)}) copy-start(bf16[2,256,1024]{2,1,0:T(8,128)(2,1)} %w_in.7) | copy-start | bytes 3145732
  17.6 15.1 %copy-start.1 = (bf16[2,256,1024]{2,1,0:T(8,128)(2,1)S(1)}, bf16[2,256,1024]{2,1,0:T(8,128)(2,1)}, u32[]{:S(2)}) copy-start(bf16[2,256,1024]{2,1,0:T(8,128)(2,1)} %w_rec.7) | copy-start | bytes 3145732
  17.6 15.1 %copy-start.5 = (f32[2,1024]{1,0:T(2,128)S(1)}, f32[2,1024]{1,0:T(2,128)}, u32[]{:S(2)}) copy-start(f32[2,1024]{1,0:T(2,128)} %gate_bias.7) | copy-start | bytes 24580
  20.0 7.2 %collective-permute-start.3 = (bf16[384,256]{1,0:T(8,128)(2,1)S(1)}, bf16[384,256]{1,0:T(8,128)(2,1)S(1)}, u32[]{:S(2)}, u32[]{:S(2)}) collective-permute-start(bf16[384,256]{1,0:T(8,128)(2,1)S(1)} %get-tuple-element.53), channel_id=1, source_target_pairs={{0,4},{1,5},{2,6},{3,7},{4,0},{5,1},{6,2},{7,3},{8,12},{9,13},{10,... | collective-permute-start | bytes 589832 | tf_op jit(solution)/shard_map/ppermute | solution.py:257
  21.8 7.8 %collective-permute-start.4 = (bf16[384,256]{1,0:T(8,128)(2,1)S(1)}, bf16[384,256]{1,0:T(8,128)(2,1)S(1)}, u32[]{:S(2)}, u32[]{:S(2)}) collective-permute-start(bf16[384,256]{1,0:T(8,128)(2,1)S(1)} %get-tuple-element.54), channel_id=1, source_target_pairs={{0,8},{1,9},{2,10},{3,11},{4,12},{5,13},{6,14},{7,15},{8,0},{9,1},... | collective-permute-start | bytes 589832 | tf_op jit(solution)/shard_map/ppermute | solution.py:257
  23.1 9.6 %collective-permute-start.5 = (bf16[384,256]{1,0:T(8,128)(2,1)S(1)}, bf16[384,256]{1,0:T(8,128)(2,1)S(1)}, u32[]{:S(2)}, u32[]{:S(2)}) collective-permute-start(bf16[384,256]{1,0:T(8,128)(2,1)S(1)} %get-tuple-element.55), channel_id=1, source_target_pairs={{0,12},{1,13},{2,14},{3,15},{4,8},{5,9},{6,10},{7,11},{8,4},{9,5},... | collective-permute-start | bytes 589832 | tf_op jit(solution)/shard_map/ppermute | solution.py:257
  32.7 6.7 %copy-start.3 = (bf16[1,32,128,128]{3,2,1,0:T(8,128)(2,1)S(1)}, bf16[1,32,128,128]{3,2,1,0:T(8,128)(2,1)}, u32[]{:S(2)}) copy-start(bf16[1,32,128,128]{3,2,1,0:T(8,128)(2,1)} %values.5) | copy-start | bytes 3145732
  33.3 2.0 %collective-permute-start.6 = (bf16[384,256]{1,0:T(8,128)(2,1)S(1)}, bf16[384,256]{1,0:T(8,128)(2,1)S(1)}, u32[]{:S(2)}, u32[]{:S(2)}) collective-permute-start(bf16[384,256]{1,0:T(8,128)(2,1)S(1)} %get-tuple-element.57), channel_id=1, source_target_pairs={{0,4},{1,5},{2,6},{3,7},{4,0},{5,1},{6,2},{7,3},{8,12},{9,13},{10,... | collective-permute-start | bytes 589832 | tf_op jit(solution)/shard_map/ppermute | solution.py:257
  34.0 1.4 copy-start.7
  34.0 1.4 collective-permute-start.7
  34.7 0.7 collective-permute-start.8
  36.0 3.4 %collective-permute-start.9 = (bf16[512,256]{1,0:T(8,128)(2,1)S(1)}, bf16[512,256]{1,0:T(8,128)(2,1)S(1)}, u32[]{:S(2)}, u32[]{:S(2)}) collective-permute-start(bf16[512,256]{1,0:T(8,128)(2,1)S(1)} %get-tuple-element.61), channel_id=1, source_target_pairs={{0,1},{1,0},{2,3},{3,2},{4,5},{5,4},{6,7},{7,6},{8,9},{9,8},{10,11... | collective-permute-start | bytes 786440 | tf_op jit(solution)/shard_map/ppermute | solution.py:257
  36.7 2.7 %collective-permute-start.10 = (bf16[512,256]{1,0:T(8,128)(2,1)S(1)}, bf16[512,256]{1,0:T(8,128)(2,1)S(1)}, u32[]{:S(2)}, u32[]{:S(2)}) collective-permute-start(bf16[512,256]{1,0:T(8,128)(2,1)S(1)} %get-tuple-element.62), channel_id=1, source_target_pairs={{0,2},{1,3},{2,0},{3,1},{4,6},{5,7},{6,4},{7,5},{8,10},{9,11},{10,... | collective-permute-start | bytes 786440 | tf_op jit(solution)/shard_map/ppermute | solution.py:257
  37.4 2.0 %collective-permute-start.11 = (bf16[512,256]{1,0:T(8,128)(2,1)S(1)}, bf16[512,256]{1,0:T(8,128)(2,1)S(1)}, u32[]{:S(2)}, u32[]{:S(2)}) collective-permute-start(bf16[512,256]{1,0:T(8,128)(2,1)S(1)} %get-tuple-element.63), channel_id=1, source_target_pairs={{0,3},{1,2},{2,1},{3,0},{4,7},{5,6},{6,5},{7,4},{8,11},{9,10},{10,... | collective-permute-start | bytes 786440 | tf_op jit(solution)/shard_map/ppermute | solution.py:257
  38.1 40.8 %collective-permute-start.18 = (bf16[2,384,256]{2,1,0:T(8,128)(2,1)S(1)}, bf16[2,384,256]{2,1,0:T(8,128)(2,1)S(1)}, u32[]{:S(2)}, u32[]{:S(2)}) collective-permute-start(bf16[2,384,256]{2,1,0:T(8,128)(2,1)S(1)} %get-tuple-element.72), channel_id=1, source_target_pairs={{0,24},{1,25},{2,26},{3,27},{4,28},{5,29},{6,30},{7,31},{8,16},{9,... | collective-permute-start | bytes 1179656 | tf_op jit(solution)/shard_map/ppermute | solution.py:257
  40.0 2.0 %collective-permute-start.12 = (bf16[384,256]{1,0:T(8,128)(2,1)S(1)}, bf16[384,256]{1,0:T(8,128)(2,1)S(1)}, u32[]{:S(2)}, u32[]{:S(2)}) collective-permute-start(bf16[384,256]{1,0:T(8,128)(2,1)S(1)} %get-tuple-element.65), channel_id=1, source_target_pairs={{0,4},{1,5},{2,6},{3,7},{4,0},{5,1},{6,2},{7,3},{8,12},{9,13},{10,... | collective-permute-start | bytes 589832 | tf_op jit(solution)/shard_map/ppermute | solution.py:257
  40.7 1.4 collective-permute-start.13
  41.4 0.7 collective-permute-start.14
  82.5 9.2 %collective-permute-start.19 = (bf16[384,256]{1,0:T(8,128)(2,1)S(1)}, bf16[384,256]{1,0:T(8,128)(2,1)S(1)}, u32[]{:S(2)}, u32[]{:S(2)}) collective-permute-start(bf16[384,256]{1,0:T(8,128)(2,1)S(1)} %get-tuple-element.75), channel_id=1, source_target_pairs={{16,20},{17,21},{18,22},{19,23},{20,16},{21,17},{22,18},{23,19},{2... | collective-permute-start | bytes 589832 | tf_op jit(solution)/shard_map/ppermute | solution.py:257
  86.1 9.7 %collective-permute-start.20 = (bf16[384,256]{1,0:T(8,128)(2,1)S(1)}, bf16[384,256]{1,0:T(8,128)(2,1)S(1)}, u32[]{:S(2)}, u32[]{:S(2)}) collective-permute-start(bf16[384,256]{1,0:T(8,128)(2,1)S(1)} %get-tuple-element.76), channel_id=1, source_target_pairs={{16,24},{17,25},{18,26},{19,27},{20,28},{21,29},{22,30},{23,31},{2... | collective-permute-start | bytes 589832 | tf_op jit(solution)/shard_map/ppermute | solution.py:257
  88.0 10.2 %collective-permute-start.21 = (bf16[384,256]{1,0:T(8,128)(2,1)S(1)}, bf16[384,256]{1,0:T(8,128)(2,1)S(1)}, u32[]{:S(2)}, u32[]{:S(2)}) collective-permute-start(bf16[384,256]{1,0:T(8,128)(2,1)S(1)} %get-tuple-element.77), channel_id=1, source_target_pairs={{16,28},{17,29},{18,30},{19,31},{20,24},{21,25},{22,26},{23,27},{2... | collective-permute-start | bytes 589832 | tf_op jit(solution)/shard_map/ppermute | solution.py:257
  98.9 8.9 %collective-permute-start.22 = (bf16[512,256]{1,0:T(8,128)(2,1)S(1)}, bf16[512,256]{1,0:T(8,128)(2,1)S(1)}, u32[]{:S(2)}, u32[]{:S(2)}) collective-permute-start(bf16[512,256]{1,0:T(8,128)(2,1)S(1)} %get-tuple-element.79), channel_id=1, source_target_pairs={{16,17},{17,16},{18,19},{19,18},{20,21},{21,20},{22,23},{23,22},{2... | collective-permute-start | bytes 786440 | tf_op jit(solution)/shard_map/ppermute | solution.py:257
  100.8 11.1 %collective-permute-start.23 = (bf16[512,256]{1,0:T(8,128)(2,1)S(1)}, bf16[512,256]{1,0:T(8,128)(2,1)S(1)}, u32[]{:S(2)}, u32[]{:S(2)}) collective-permute-start(bf16[512,256]{1,0:T(8,128)(2,1)S(1)} %get-tuple-element.80), channel_id=1, source_target_pairs={{16,18},{17,19},{18,16},{19,17},{20,22},{21,23},{22,20},{23,21},{2... | collective-permute-start | bytes 786440 | tf_op jit(solution)/shard_map/ppermute | solution.py:257
  103.7 12.9 %collective-permute-start.24 = (bf16[512,256]{1,0:T(8,128)(2,1)S(1)}, bf16[512,256]{1,0:T(8,128)(2,1)S(1)}, u32[]{:S(2)}, u32[]{:S(2)}) collective-permute-start(bf16[512,256]{1,0:T(8,128)(2,1)S(1)} %get-tuple-element.81), channel_id=1, source_target_pairs={{16,19},{17,18},{18,17},{19,16},{20,23},{21,22},{22,21},{23,20},{2... | collective-permute-start | bytes 786440 | tf_op jit(solution)/shard_map/ppermute | solution.py:257
  106.5 22.4 %collective-permute-start.28 = (bf16[2,384,256]{2,1,0:T(8,128)(2,1)S(1)}, bf16[2,384,256]{2,1,0:T(8,128)(2,1)S(1)}, u32[]{:S(2)}, u32[]{:S(2)}) collective-permute-start(bf16[2,384,256]{2,1,0:T(8,128)(2,1)S(1)} %get-tuple-element.86), channel_id=1, source_target_pairs={{0,24},{1,25},{2,26},{3,27},{4,28},{5,29},{6,30},{7,31},{8,16},{9,... | collective-permute-start | bytes 1179656 | tf_op jit(solution)/shard_map/ppermute | solution.py:257
  119.0 10.6 %collective-permute-start.25 = (bf16[384,256]{1,0:T(8,128)(2,1)S(1)}, bf16[384,256]{1,0:T(8,128)(2,1)S(1)}, u32[]{:S(2)}, u32[]{:S(2)}) collective-permute-start(bf16[384,256]{1,0:T(8,128)(2,1)S(1)} %get-tuple-element.83), channel_id=1, source_target_pairs={{16,20},{17,21},{18,22},{19,23},{20,16},{21,17},{22,18},{23,19},{2... | collective-permute-start | bytes 589832 | tf_op jit(solution)/shard_map/ppermute | solution.py:257
  122.9 9.7 %collective-permute-start.26 = (bf16[384,256]{1,0:T(8,128)(2,1)S(1)}, bf16[384,256]{1,0:T(8,128)(2,1)S(1)}, u32[]{:S(2)}, u32[]{:S(2)}) collective-permute-start(bf16[384,256]{1,0:T(8,128)(2,1)S(1)} %get-tuple-element.84), channel_id=1, source_target_pairs={{16,24},{17,25},{18,26},{19,27},{20,28},{21,29},{22,30},{23,31},{2... | collective-permute-start | bytes 589832 | tf_op jit(solution)/shard_map/ppermute | solution.py:257
  124.9 11.0 %collective-permute-start.27 = (bf16[384,256]{1,0:T(8,128)(2,1)S(1)}, bf16[384,256]{1,0:T(8,128)(2,1)S(1)}, u32[]{:S(2)}, u32[]{:S(2)}) collective-permute-start(bf16[384,256]{1,0:T(8,128)(2,1)S(1)} %get-tuple-element.85), channel_id=1, source_target_pairs={{16,28},{17,29},{18,30},{19,31},{20,24},{21,25},{22,26},{23,27},{2... | collective-permute-start | bytes 589832 | tf_op jit(solution)/shard_map/ppermute | solution.py:257
  128.2 17.1 %collective-permute-start.15 = (bf16[384,256]{1,0:T(8,128)(2,1)S(1)}, bf16[384,256]{1,0:T(8,128)(2,1)S(1)}, u32[]{:S(2)}, u32[]{:S(2)}) collective-permute-start(bf16[384,256]{1,0:T(8,128)(2,1)S(1)} %get-tuple-element.69), channel_id=1, source_target_pairs={{0,4},{1,5},{2,6},{3,7},{4,0},{5,1},{6,2},{7,3},{8,12},{9,13},{10,... | collective-permute-start | bytes 589832 | tf_op jit(solution)/shard_map/ppermute | solution.py:257
  128.9 19.7 %collective-permute-start.16 = (bf16[384,256]{1,0:T(8,128)(2,1)S(1)}, bf16[384,256]{1,0:T(8,128)(2,1)S(1)}, u32[]{:S(2)}, u32[]{:S(2)}) collective-permute-start(bf16[384,256]{1,0:T(8,128)(2,1)S(1)} %get-tuple-element.70), channel_id=1, source_target_pairs={{0,8},{1,9},{2,10},{3,11},{4,12},{5,13},{6,14},{7,15},{8,0},{9,1},... | collective-permute-start | bytes 589832 | tf_op jit(solution)/shard_map/ppermute | solution.py:257
  129.6 19.1 %collective-permute-start.17 = (bf16[384,256]{1,0:T(8,128)(2,1)S(1)}, bf16[384,256]{1,0:T(8,128)(2,1)S(1)}, u32[]{:S(2)}, u32[]{:S(2)}) collective-permute-start(bf16[384,256]{1,0:T(8,128)(2,1)S(1)} %get-tuple-element.71), channel_id=1, source_target_pairs={{0,12},{1,13},{2,14},{3,15},{4,8},{5,9},{6,10},{7,11},{8,4},{9,5},... | collective-permute-start | bytes 589832 | tf_op jit(solution)/shard_map/ppermute | solution.py:257
  139.4 9.3 %collective-permute-start.29 = (bf16[384,256]{1,0:T(8,128)(2,1)S(1)}, bf16[384,256]{1,0:T(8,128)(2,1)S(1)}, u32[]{:S(2)}, u32[]{:S(2)}) collective-permute-start(bf16[384,256]{1,0:T(8,128)(2,1)S(1)} %get-tuple-element.88), channel_id=1, source_target_pairs={{16,20},{17,21},{18,22},{19,23},{20,16},{21,17},{22,18},{23,19},{2... | collective-permute-start | bytes 589832 | tf_op jit(solution)/shard_map/ppermute | solution.py:257
  143.1 9.7 %collective-permute-start.30 = (bf16[384,256]{1,0:T(8,128)(2,1)S(1)}, bf16[384,256]{1,0:T(8,128)(2,1)S(1)}, u32[]{:S(2)}, u32[]{:S(2)}) collective-permute-start(bf16[384,256]{1,0:T(8,128)(2,1)S(1)} %get-tuple-element.89), channel_id=1, source_target_pairs={{16,24},{17,25},{18,26},{19,27},{20,28},{21,29},{22,30},{23,31},{2... | collective-permute-start | bytes 589832 | tf_op jit(solution)/shard_map/ppermute | solution.py:257
  145.3 9.8 %collective-permute-start.31 = (bf16[384,256]{1,0:T(8,128)(2,1)S(1)}, bf16[384,256]{1,0:T(8,128)(2,1)S(1)}, u32[]{:S(2)}, u32[]{:S(2)}) collective-permute-start(bf16[384,256]{1,0:T(8,128)(2,1)S(1)} %get-tuple-element.90), channel_id=1, source_target_pairs={{16,28},{17,29},{18,30},{19,31},{20,24},{21,25},{22,26},{23,27},{2... | collective-permute-start | bytes 589832 | tf_op jit(solution)/shard_map/ppermute | solution.py:257
